TPU v7x, 32 devices: a whole 2x2x4 slice. The times are simulated.
32 devices in a mesh: blk: 8 (over z, x), aux: 4 (over y, core).
Axes of the slice: x: 2, y: 2, z: 4, core: 2. Of those that a mesh axis runs over, the one named last changes fastest.
Arguments:
- half_ints: bfloat16 [32, 1536, 384], P('blk', 'aux'), may hold values from -0.625 to 0.625
- metric_inv: bfloat16 [1536, 1536], P('aux'), may hold values from -1 to 2, as said below
- occ_energy: float32 [32], replicated, may hold values from -2 to -0.3
- vir_energy: float32 [384], replicated, may hold values from 0.3 to 3
Outputs:
- gamma: bfloat16 [32, 1536, 384], P('blk', 'aux')
Inputs may be any that keep to these rules, and one draw needn't show every extreme that they name: metric_inv is lower triangular (zero where Q > P) with a positive diagonal.
All inputs are finite; a program needn't handle non-finite values.
Results may differ from a plain program's by a relative error of at most 0.0058.
Values may be sent and summed in bfloat16 or wider, within the bound.
A program may use at most 64 MiB of HBM per device.

v0:
```python
import functools

import jax
import jax.numpy as jnp
from jax import lax
from jax.experimental import pallas as pl
from jax.experimental.pallas import tpu as pltpu
from jax.sharding import PartitionSpec as P

CYCLE = 4
MESH = pl.DeviceIdType.MESH


def kernel(
    blocks, groups, tile,
    ints_ref, metric_ref, occ_ref, vir_ref,
    out_ref,
    ints, metric, metric_t, fit, fit_t, gap, dens, dens_b, gam,
    h_send, h_recv, z_send, c_send, f_send, w_send, ring_recv,
    m1_send, m1_recv, m2_send, m2_recv, m3_send, m3_recv, own_sem, g_send, g_recv,
):
    shard = ints_ref.shape[1]
    half = shard // 2
    parts = 4 if half % 64 == 0 else 1
    part = half // parts
    naux = metric_ref.shape[1]
    vir = ints_ref.shape[2]
    tiles = naux // tile
    pairs = groups // 2
    b, g = lax.axis_index("blk"), lax.axis_index("aux")
    x, core, h = b % 2, g % 2, g // 2
    plane, mate, ahead = b - x, g + 1 - 2 * core, (b + 2) % blocks
    across = b + 1 - 2 * x
    own_b, own_c = plane + core, g - core + x

    def rows(p):
        return pl.ds(pl.multiple_of(p * shard, shard), shard)

    def slab(p, which, n):
        return pl.ds(pl.multiple_of(p * shard + which * half + n * part, part), part)

    def width(hv):
        return min(naux, -(-2 * shard * (hv + 1) // tile) * tile)

    def remote(src, dst, send, recv, device):
        return pltpu.make_async_remote_copy(
            src_ref=src, dst_ref=dst, send_sem=send, recv_sem=recv,
            device_id=device, device_id_type=MESH,
        )

    def landed(dst, recv):
        pltpu.make_async_copy(dst, dst, recv).wait()

    barrier = pltpu.get_barrier_semaphore()
    for xx in range(2):
        for gg in range(groups):
            @pl.when((plane + xx != b) | (gg != g))
            def _():
                pl.semaphore_signal(barrier, inc=1, device_id=(plane + xx, gg), device_id_type=MESH)
    for bb in (ahead, (b + blocks - 2) % blocks):
        for gg in (g, mate):
            pl.semaphore_signal(barrier, inc=1, device_id=(bb, gg), device_id_type=MESH)
    pl.semaphore_wait(barrier, 2 * groups + 3)

    def ints_copy(c):
        return remote(
            ints_ref.at[c], ints.at[0, rows(g)], h_send.at[c], h_recv.at[g],
            (plane + c % 2, c - c % 2 + x),
        )

    def to_self(c):
        return (core == x) & (c == own_c)

    order = [(2 * ((h + r) % pairs) + par) for r in range(pairs) for par in range(2)]
    own_metric = pltpu.make_async_copy(metric_ref, metric.at[rows(g)], own_sem)
    own_metric.start()

    def m1_copy(hv, r, n):
        return remote(
            metric_ref.at[slab(0, x, n), pl.ds(0, width(hv))],
            metric.at[slab(g, x, n), pl.ds(0, width(hv))],
            m1_send.at[r, n], m1_recv.at[hv, n],
            (b, 2 * ((h + r) % pairs) + core),
        )

    def m3_own(hv):
        return remote(
            metric_ref.at[:, pl.ds(0, width(hv))], metric.at[rows(g), pl.ds(0, width(hv))],
            m3_send.at[hv], m3_recv.at[hv], (b, mate),
        )

    def m2_copy(hv, n):
        piece = metric.at[slab(2 * hv + core, x, n), pl.ds(0, width(hv))]
        return remote(piece, piece, m2_send.at[hv, n], m2_recv.at[hv, n], (across, g))

    def m3_copy(hv):
        piece = metric.at[rows(2 * hv + core), pl.ds(0, width(hv))]
        return remote(piece, piece, m3_send.at[hv], m3_recv.at[hv], (b, mate))

    for hv in range(pairs):
        @pl.when(h == hv)
        def _():
            for r in range(1, pairs):
                for n in range(parts):
                    m1_copy(hv, r, n).start()
            m3_own(hv).start()

    for c in order:
        @pl.when(jnp.logical_not(to_self(c)))
        def _():
            ints_copy(c).start()

        @pl.when(to_self(c))
        def _():
            pltpu.make_async_copy(ints_ref.at[c], ints.at[0, rows(g)], h_recv.at[g]).start()

    def z_copy(p):
        return remote(ints.at[0, rows(p)], ints.at[2, rows(p)], z_send.at[p], ring_recv.at[2, p], (ahead, g))

    def c_copy(p):
        return remote(ints.at[0, rows(p)], ints.at[1, rows(p)], c_send.at[p], ring_recv.at[1, p], (b, mate))

    def f_copy(p, role):
        return remote(ints.at[2, rows(p)], ints.at[role, rows(p)], f_send.at[p], ring_recv.at[role, p], (b, mate))

    def w_copy(p):
        return remote(ints.at[2, rows(p)], ints.at[3, rows(p)], w_send.at[p], ring_recv.at[3, p], (ahead, mate))

    def pass_own(p):
        landed(ints.at[0, rows(p)], h_recv.at[p])
        z_copy(p).start()

        @pl.when(core == 0)
        def _():
            c_copy(p).start()

    def pass_on(p):
        landed(ints.at[2, rows(p)], ring_recv.at[2, p])

        @pl.when(core == 1)
        def _():
            w_copy(p).start()
            f_copy(p, 1).start()

        @pl.when(core == 0)
        def _():
            f_copy(p, 3).start()

    for p in order[:2]:
        pass_own(p)
    for hv in range(pairs):
        @pl.when(h != hv)
        def _():
            for n in range(parts):
                landed(metric.at[slab(2 * hv + core, x, n), pl.ds(0, width(hv))], m1_recv.at[hv, n])
                m2_copy(hv, n).start()
    for p in order[:2]:
        pass_on(p)
    for hv in range(pairs):
        @pl.when(h != hv)
        def _():
            for n in range(parts):
                landed(metric.at[slab(2 * hv + core, 1 - x, n), pl.ds(0, width(hv))], m2_recv.at[hv, n])
            m3_copy(hv).start()
    for p in order[2:]:
        pass_own(p)

    own_metric.wait()
    for hv in range(pairs):
        landed(metric.at[rows(2 * hv + 1 - core), pl.ds(0, width(hv))], m3_recv.at[hv])

    levels = jnp.broadcast_to(vir_ref[...], (vir, vir))
    gap[...] = levels + levels.T

    def span(q):
        return pl.ds(pl.multiple_of(q * tile, tile), tile)

    @pl.loop(0, tiles)
    def _(p):
        @pl.loop(0, p + 1)
        def _(q):
            metric_t[span(q), span(p)] = metric[span(p), span(q)].T

    own_energy = occ_ref[own_b * groups + own_c]

    @pl.loop(0, CYCLE)
    def _(k):
        role = (k % 2) * 2 + k // 2

        @pl.when(k == 1)
        def _():
            for p in order[2:]:
                pass_on(p)

        @pl.when(role % 2 == 1)
        def _():
            for p in range(groups):
                landed(ints.at[role, rows(p)], ring_recv.at[role, p])

        for q in range(tiles):
            low = q * tile
            fit[low:low + tile, :] = jnp.dot(
                metric_t[low:low + tile, low:], ints[role, low:, :],
                preferred_element_type=jnp.float32,
            ).astype(fit.dtype)

        @pl.when(k == 0)
        def _():
            @pl.loop(0, tiles)
            def _(q):
                fit_t[:, span(q)] = fit[span(q), :].T

        pair = jnp.dot(fit_t[...], fit[...], preferred_element_type=jnp.float32)
        energy = own_energy + occ_ref[(own_b + blocks - role) % blocks * groups + own_c]
        amplitude_t = ((2.0 * pair.T - pair) / (energy - gap[...])).astype(fit.dtype)

        @pl.when(k == 0)
        def _():
            dens[...] = jnp.dot(fit[...], amplitude_t, preferred_element_type=jnp.float32)

        @pl.when((k > 0) & (k < CYCLE - 1))
        def _():
            dens[...] += jnp.dot(fit[...], amplitude_t, preferred_element_type=jnp.float32)

        @pl.when(k == CYCLE - 1)
        def _():
            total = dens[...] + jnp.dot(fit[...], amplitude_t, preferred_element_type=jnp.float32)
            dens_b[...] = total.astype(dens_b.dtype)

    def g_copy(p):
        return remote(gam.at[rows(p)], out_ref.at[own_c], g_send.at[p], g_recv.at[own_c], (own_b, p))

    def g_self(p):
        return (core == x) & (g == p)

    for t in range(tiles):
        low = t * tile
        gam[low:low + tile, :] = jnp.dot(
            metric[low:low + tile, :low + tile], dens_b[:low + tile, :],
            preferred_element_type=jnp.float32,
        ).astype(gam.dtype)
        for p in range(low // shard, (low + tile) // shard):
            @pl.when(jnp.logical_not(g_self(p)))
            def _():
                g_copy(p).start()

            @pl.when(g_self(p))
            def _():
                pltpu.make_async_copy(gam.at[rows(p)], out_ref.at[own_c], g_recv.at[own_c]).start()

    for c in range(groups):
        @pl.when(jnp.logical_not(to_self(c)))
        def _():
            ints_copy(c).wait_send()
        z_copy(c).wait_send()

        @pl.when(core == 0)
        def _():
            c_copy(c).wait_send()
        f_copy(c, 1).wait_send()

        @pl.when(core == 1)
        def _():
            w_copy(c).wait_send()

        @pl.when(jnp.logical_not(g_self(c)))
        def _():
            g_copy(c).wait_send()
    for hv in range(pairs):
        @pl.when(h == hv)
        def _():
            for r in range(1, pairs):
                for n in range(parts):
                    m1_copy(hv, r, n).wait_send()
            m3_own(hv).wait_send()

        @pl.when(h != hv)
        def _():
            for n in range(parts):
                m2_copy(hv, n).wait_send()
            m3_copy(hv).wait_send()
    for c in range(groups):
        landed(out_ref.at[c], g_recv.at[c])


def local(half_ints, metric_inv, occ_energy, vir_energy):
    groups, blocks = lax.axis_size("aux"), lax.axis_size("blk")
    shard, vir = half_ints.shape[1:]
    naux = metric_inv.shape[1]
    tile = shard if shard % 128 == 0 else naux // 4
    pairs = groups // 2
    parts = 4 if shard % 128 == 0 else 1
    dma = pltpu.SemaphoreType.DMA
    return pl.pallas_call(
        functools.partial(kernel, blocks, groups, tile),
        out_shape=jax.ShapeDtypeStruct(half_ints.shape, jnp.bfloat16),
        in_specs=[
            pl.BlockSpec(memory_space=pl.ANY),
            pl.BlockSpec(memory_space=pl.ANY),
            pl.BlockSpec(memory_space=pltpu.SMEM),
            pl.BlockSpec(memory_space=pltpu.VMEM),
        ],
        out_specs=pl.BlockSpec(memory_space=pl.ANY),
        scratch_shapes=[
            pltpu.VMEM((CYCLE, naux, vir), jnp.bfloat16),
            pltpu.VMEM((naux, naux), jnp.bfloat16),
            pltpu.VMEM((naux, naux), jnp.bfloat16),
            pltpu.VMEM((naux, vir), jnp.bfloat16),
            pltpu.VMEM((vir, naux), jnp.bfloat16),
            pltpu.VMEM((vir, vir), jnp.float32),
            pltpu.VMEM((naux, vir), jnp.float32),
            pltpu.VMEM((naux, vir), jnp.bfloat16),
            pltpu.VMEM((naux, vir), jnp.bfloat16),
            dma((groups,)), dma((groups,)), dma((groups,)), dma((groups,)), dma((groups,)),
            dma((groups,)), dma((CYCLE, groups)),
            dma((pairs, parts)), dma((pairs, parts)), dma((pairs, parts)), dma((pairs, parts)), dma((pairs,)), dma((pairs,)),
            dma(()), dma((groups,)), dma((groups,)),
        ],
        compiler_params=pltpu.CompilerParams(
            collective_id=0, has_side_effects=True, vmem_limit_bytes=56 * 2**20
        ),
    )(half_ints, metric_inv, occ_energy, vir_energy)


def solution(mesh):
    placed = (P("blk", "aux", None), P("aux", None), P(), P())
    return jax.shard_map(
        local, mesh=mesh, in_specs=placed, out_specs=P("blk", "aux", None), check_vma=False
    )
```

profile of v0, /device:TPU:0, one launch (start us, length us, event | category | flops | bytes accessed | tf_op | source)
XLA Modules:
  0.0 78.7 jit_solution(13482039766516115618)
XLA Ops:
  0.0 76.2 %shard_map.46 = bf16[4,384,384]{2,1,0:T(8,128)(2,1)} custom-call(bf16[4,384,384]{2,1,0:T(8,128)(2,1)} %ints_ref.1, bf16[384,1536]{1,0:T(8,128)(2,1)} %metric_ref.1, f32[32]{0:T(128)} %occ_ref.1, f32[384]{0:T(512)} %vir_ref.1), custom_call_target="tpu_custom_call" | custom-call | tf_op jit(solution)/shard_map/pallas_call | solution.py:294
  76.3 2.4 %copy.6 = bf16[4,384,384]{2,1,0:T(8,128)(2,1)} copy(bf16[4,384,384]{2,1,0:T(8,128)(2,1)} %shard_map.46) | data formatting | bytes 2359296
where the time goes:
time: 78.8 us; the launch traced here: 78.7 us
  Pallas kernels  76.2 us (97%)
  local copies, waits for them, and re-layouts  2.4 us (3%)
    pallas_call x1, Pallas kernels, local(): pl.pallas_call(functools.partial(kernel, blocks, groups, tile), out_shape...  76.2 us
    unnamed x1, local copies, waits for them, and re-layouts  2.4 us

commit v1 on v0

--- a/solution.py
+++ b/solution.py
@@ -15,8 +15,8 @@
     blocks, groups, tile,
     ints_ref, metric_ref, occ_ref, vir_ref,
     out_ref,
-    ints, metric, metric_t, fit, fit_t, gap, dens, dens_b, gam,
-    h_send, h_recv, z_send, c_send, f_send, w_send, ring_recv,
+    ints, metric, metric_t, fits, fit_t, gap, pair_sum, dens, dens_b, gam,
+    h_send, h_recv, d_send, z_send, w_send, ring_recv, f_send, f_recv,
     m1_send, m1_recv, m2_send, m2_recv, m3_send, m3_recv, own_sem, g_send, g_recv,
 ):
     shard = ints_ref.shape[1]
@@ -32,12 +32,16 @@
     plane, mate, ahead = b - x, g + 1 - 2 * core, (b + 2) % blocks
     across = b + 1 - 2 * x
     own_b, own_c = plane + core, g - core + x
+    f32 = jnp.float32
 
     def rows(p):
         return pl.ds(pl.multiple_of(p * shard, shard), shard)
 
     def slab(p, which, n):
         return pl.ds(pl.multiple_of(p * shard + which * half + n * part, part), part)
+
+    def span(q):
+        return pl.ds(pl.multiple_of(q * tile, tile), tile)
 
     def width(hv):
         return min(naux, -(-2 * shard * (hv + 1) // tile) * tile)
@@ -72,6 +76,23 @@
         return (core == x) & (c == own_c)
 
     order = [(2 * ((h + r) % pairs) + par) for r in range(pairs) for par in range(2)]
+    tail_first = [groups - 2] + [p for p in range(groups - 1, -1, -1) if p != groups - 2]
+
+    def d_copy():
+        return remote(
+            ints_ref.at[own_c], ints.at[2, rows(g)], d_send, ring_recv.at[2, g], (ahead, own_c)
+        )
+
+    d_copy().start()
+    for c in order:
+        @pl.when(jnp.logical_not(to_self(c)))
+        def _():
+            ints_copy(c).start()
+
+        @pl.when(to_self(c))
+        def _():
+            pltpu.make_async_copy(ints_ref.at[c], ints.at[0, rows(g)], h_recv.at[g]).start()
+
     own_metric = pltpu.make_async_copy(metric_ref, metric.at[rows(g)], own_sem)
     own_metric.start()
 
@@ -105,75 +126,51 @@
                     m1_copy(hv, r, n).start()
             m3_own(hv).start()
 
-    for c in order:
-        @pl.when(jnp.logical_not(to_self(c)))
-        def _():
-            ints_copy(c).start()
-
-        @pl.when(to_self(c))
-        def _():
-            pltpu.make_async_copy(ints_ref.at[c], ints.at[0, rows(g)], h_recv.at[g]).start()
-
     def z_copy(p):
         return remote(ints.at[0, rows(p)], ints.at[2, rows(p)], z_send.at[p], ring_recv.at[2, p], (ahead, g))
 
-    def c_copy(p):
-        return remote(ints.at[0, rows(p)], ints.at[1, rows(p)], c_send.at[p], ring_recv.at[1, p], (b, mate))
-
-    def f_copy(p, role):
-        return remote(ints.at[2, rows(p)], ints.at[role, rows(p)], f_send.at[p], ring_recv.at[role, p], (b, mate))
-
     def w_copy(p):
         return remote(ints.at[2, rows(p)], ints.at[3, rows(p)], w_send.at[p], ring_recv.at[3, p], (ahead, mate))
 
-    def pass_own(p):
+    def sent_up(p):
+        return jnp.logical_not((core == x) & (p // 2 == h))
+
+    def f_copy(src, dst):
+        return remote(fits.at[src], fits.at[dst], f_send.at[dst // 2], f_recv.at[dst // 2], (b, mate))
+
+    levels = jnp.broadcast_to(vir_ref[...], (vir, vir))
+    gap[...] = levels + levels.T
+
+    for p in order:
         landed(ints.at[0, rows(p)], h_recv.at[p])
-        z_copy(p).start()
-
-        @pl.when(core == 0)
-        def _():
-            c_copy(p).start()
-
-    def pass_on(p):
-        landed(ints.at[2, rows(p)], ring_recv.at[2, p])
-
-        @pl.when(core == 1)
-        def _():
-            w_copy(p).start()
-            f_copy(p, 1).start()
-
-        @pl.when(core == 0)
-        def _():
-            f_copy(p, 3).start()
-
-    for p in order[:2]:
-        pass_own(p)
+
+        @pl.when(sent_up(p))
+        def _():
+            z_copy(p).start()
+
     for hv in range(pairs):
         @pl.when(h != hv)
         def _():
             for n in range(parts):
                 landed(metric.at[slab(2 * hv + core, x, n), pl.ds(0, width(hv))], m1_recv.at[hv, n])
                 m2_copy(hv, n).start()
-    for p in order[:2]:
-        pass_on(p)
     for hv in range(pairs):
         @pl.when(h != hv)
         def _():
             for n in range(parts):
                 landed(metric.at[slab(2 * hv + core, 1 - x, n), pl.ds(0, width(hv))], m2_recv.at[hv, n])
             m3_copy(hv).start()
-    for p in order[2:]:
-        pass_own(p)
+
+    for p in tail_first:
+        landed(ints.at[2, rows(p)], ring_recv.at[2, p])
+
+        @pl.when(core == 1)
+        def _():
+            w_copy(p).start()
 
     own_metric.wait()
     for hv in range(pairs):
         landed(metric.at[rows(2 * hv + 1 - core), pl.ds(0, width(hv))], m3_recv.at[hv])
-
-    levels = jnp.broadcast_to(vir_ref[...], (vir, vir))
-    gap[...] = levels + levels.T
-
-    def span(q):
-        return pl.ds(pl.multiple_of(q * tile, tile), tile)
 
     @pl.loop(0, tiles)
     def _(p):
@@ -183,49 +180,73 @@
 
     own_energy = occ_ref[own_b * groups + own_c]
 
-    @pl.loop(0, CYCLE)
+    def fit_tile(role, q):
+        low = q * tile
+        fits[role, low:low + tile, :] = jnp.dot(
+            metric_t[low:low + tile, low:], ints[role, low:, :], preferred_element_type=f32,
+        ).astype(fits.dtype)
+
+    def amplitude_of(pair, role):
+        energy = own_energy + occ_ref[(own_b + blocks - role) % blocks * groups + own_c]
+        return ((2.0 * pair.T - pair) / (energy - gap[...])).astype(fits.dtype)
+
+    for role in (0, 2):
+        for q in range(tiles):
+            fit_tile(role, q)
+
+        @pl.when(core == 0)
+        def _():
+            f_copy(role, role + 1).start()
+
+        if role == 2:
+            @pl.when(core == 1)
+            def _():
+                f_copy(2, 1).start()
+
+    @pl.loop(0, tiles)
+    def _(q):
+        fit_t[:, span(q)] = fits[0, span(q), :].T
+
+    @pl.loop(0, CYCLE - 1)
     def _(k):
-        role = (k % 2) * 2 + k // 2
-
-        @pl.when(k == 1)
-        def _():
-            for p in order[2:]:
-                pass_on(p)
-
-        @pl.when(role % 2 == 1)
-        def _():
-            for p in range(groups):
-                landed(ints.at[role, rows(p)], ring_recv.at[role, p])
-
-        for q in range(tiles):
+        role = 2 * k - 3 * (k // 2)
+
+        @pl.when(k == 2)
+        def _():
+            landed(fits.at[1], f_recv.at[0])
+
+        pair = jnp.dot(fit_t[...], fits[role], preferred_element_type=f32)
+        amplitude_t = amplitude_of(pair, role)
+
+        @pl.when(k == 0)
+        def _():
+            dens[...] = jnp.dot(fits[role], amplitude_t, preferred_element_type=f32)
+
+        @pl.when(k > 0)
+        def _():
+            dens[...] += jnp.dot(fits[role], amplitude_t, preferred_element_type=f32)
+
+    @pl.when(core == 1)
+    def _():
+        landed(fits.at[3], f_recv.at[1])
+        pair_sum[...] = jnp.dot(fit_t[...], fits[3], preferred_element_type=f32)
+
+    @pl.when(core == 0)
+    def _():
+        for q in reversed(range(tiles)):
             low = q * tile
-            fit[low:low + tile, :] = jnp.dot(
-                metric_t[low:low + tile, low:], ints[role, low:, :],
-                preferred_element_type=jnp.float32,
-            ).astype(fit.dtype)
-
-        @pl.when(k == 0)
-        def _():
-            @pl.loop(0, tiles)
-            def _(q):
-                fit_t[:, span(q)] = fit[span(q), :].T
-
-        pair = jnp.dot(fit_t[...], fit[...], preferred_element_type=jnp.float32)
-        energy = own_energy + occ_ref[(own_b + blocks - role) % blocks * groups + own_c]
-        amplitude_t = ((2.0 * pair.T - pair) / (energy - gap[...])).astype(fit.dtype)
-
-        @pl.when(k == 0)
-        def _():
-            dens[...] = jnp.dot(fit[...], amplitude_t, preferred_element_type=jnp.float32)
-
-        @pl.when((k > 0) & (k < CYCLE - 1))
-        def _():
-            dens[...] += jnp.dot(fit[...], amplitude_t, preferred_element_type=jnp.float32)
-
-        @pl.when(k == CYCLE - 1)
-        def _():
-            total = dens[...] + jnp.dot(fit[...], amplitude_t, preferred_element_type=jnp.float32)
-            dens_b[...] = total.astype(dens_b.dtype)
+            for p in reversed(range(low // shard, (low + tile) // shard)):
+                landed(ints.at[3, rows(p)], ring_recv.at[3, p])
+            fit_tile(3, q)
+            part_sum = jnp.dot(
+                fit_t[:, low:low + tile], fits[3, low:low + tile, :], preferred_element_type=f32
+            )
+            if q == tiles - 1:
+                pair_sum[...] = part_sum
+            else:
+                pair_sum[...] += part_sum
+
+    amplitude_t = amplitude_of(pair_sum[...], 3)
 
     def g_copy(p):
         return remote(gam.at[rows(p)], out_ref.at[own_c], g_send.at[p], g_recv.at[own_c], (own_b, p))
@@ -235,9 +256,13 @@
 
     for t in range(tiles):
         low = t * tile
+        total = dens[low:low + tile, :] + jnp.dot(
+            fits[3, low:low + tile, :], amplitude_t, preferred_element_type=f32
+        )
+        dens_b[low:low + tile, :] = total.astype(dens_b.dtype)
         gam[low:low + tile, :] = jnp.dot(
             metric[low:low + tile, :low + tile], dens_b[:low + tile, :],
-            preferred_element_type=jnp.float32,
+            preferred_element_type=f32,
         ).astype(gam.dtype)
         for p in range(low // shard, (low + tile) // shard):
             @pl.when(jnp.logical_not(g_self(p)))
@@ -248,16 +273,15 @@
             def _():
                 pltpu.make_async_copy(gam.at[rows(p)], out_ref.at[own_c], g_recv.at[own_c]).start()
 
+    d_copy().wait_send()
     for c in range(groups):
         @pl.when(jnp.logical_not(to_self(c)))
         def _():
             ints_copy(c).wait_send()
-        z_copy(c).wait_send()
-
-        @pl.when(core == 0)
-        def _():
-            c_copy(c).wait_send()
-        f_copy(c, 1).wait_send()
+
+        @pl.when(sent_up(c))
+        def _():
+            z_copy(c).wait_send()
 
         @pl.when(core == 1)
         def _():
@@ -266,6 +290,16 @@
         @pl.when(jnp.logical_not(g_self(c)))
         def _():
             g_copy(c).wait_send()
+
+    @pl.when(core == 0)
+    def _():
+        f_copy(0, 1).wait_send()
+        f_copy(2, 3).wait_send()
+
+    @pl.when(core == 1)
+    def _():
+        f_copy(2, 1).wait_send()
+
     for hv in range(pairs):
         @pl.when(h == hv)
         def _():
@@ -305,14 +339,15 @@
             pltpu.VMEM((CYCLE, naux, vir), jnp.bfloat16),
             pltpu.VMEM((naux, naux), jnp.bfloat16),
             pltpu.VMEM((naux, naux), jnp.bfloat16),
-            pltpu.VMEM((naux, vir), jnp.bfloat16),
+            pltpu.VMEM((CYCLE, naux, vir), jnp.bfloat16),
             pltpu.VMEM((vir, naux), jnp.bfloat16),
+            pltpu.VMEM((vir, vir), jnp.float32),
             pltpu.VMEM((vir, vir), jnp.float32),
             pltpu.VMEM((naux, vir), jnp.float32),
             pltpu.VMEM((naux, vir), jnp.bfloat16),
             pltpu.VMEM((naux, vir), jnp.bfloat16),
-            dma((groups,)), dma((groups,)), dma((groups,)), dma((groups,)), dma((groups,)),
-            dma((groups,)), dma((CYCLE, groups)),
+            dma((groups,)), dma((groups,)), dma(()), dma((groups,)), dma((groups,)), dma((CYCLE, groups)),
+            dma((2,)), dma((2,)),
             dma((pairs, parts)), dma((pairs, parts)), dma((pairs, parts)), dma((pairs, parts)), dma((pairs,)), dma((pairs,)),
             dma(()), dma((groups,)), dma((groups,)),
         ],

time: 78.8 us -> 74 us (0.939)
  Pallas kernels: 76.2 us -> 71.4 us
    pallas_call x1, Pallas kernels: 76.2 us -> 71.4 us  [local(): pl.pallas_call(functools.partial(kernel, blocks, groups, tile), out_shape...]
where the time goes in v1:
time: 74 us; the launch traced here: 73.8 us
  Pallas kernels  71.4 us (96%)
  local copies, waits for them, and re-layouts  2.4 us (3%)
    pallas_call x1, Pallas kernels, local(): pl.pallas_call(functools.partial(kernel, blocks, groups, tile), out_shape...  71.4 us
    unnamed x1, local copies, waits for them, and re-layouts  2.4 us

profile of v1, /device:TPU:0, one launch (start us, length us, event | category | flops | bytes accessed | tf_op | source)
XLA Modules:
  0.0 73.8 jit_solution(868337548717991287)
XLA Ops:
  0.0 71.4 %shard_map.46 = bf16[4,384,384]{2,1,0:T(8,128)(2,1)} custom-call(bf16[4,384,384]{2,1,0:T(8,128)(2,1)} %ints_ref.1, bf16[384,1536]{1,0:T(8,128)(2,1)} %metric_ref.1, f32[32]{0:T(128)} %occ_ref.1, f32[384]{0:T(512)} %vir_ref.1), custom_call_target="tpu_custom_call" | custom-call | tf_op jit(solution)/shard_map/pallas_call | solution.py:328
  71.4 2.4 %copy.6 = bf16[4,384,384]{2,1,0:T(8,128)(2,1)} copy(bf16[4,384,384]{2,1,0:T(8,128)(2,1)} %shard_map.46) | data formatting | bytes 2359296

commit v2 on v1

--- a/solution.py
+++ b/solution.py
@@ -7,7 +7,6 @@
 from jax.experimental.pallas import tpu as pltpu
 from jax.sharding import PartitionSpec as P
 
-CYCLE = 4
 MESH = pl.DeviceIdType.MESH
 
 
@@ -15,8 +14,8 @@
     blocks, groups, tile,
     ints_ref, metric_ref, occ_ref, vir_ref,
     out_ref,
-    ints, metric, metric_t, fits, fit_t, gap, pair_sum, dens, dens_b, gam,
-    h_send, h_recv, d_send, z_send, w_send, ring_recv, f_send, f_recv,
+    near, far, metric, metric_t, fit_a, fit_b, fit_t, amp_a, amp_b, gap, pair_sum, dens, dens_b, gam, occ, levels,
+    occ_sem, vir_sem, h_send, h_recv, d_send, z_send, w_send, ring_recv, f_send, f_recv,
     m1_send, m1_recv, m2_send, m2_recv, m3_send, m3_recv, own_sem, g_send, g_recv,
 ):
     shard = ints_ref.shape[1]
@@ -55,6 +54,9 @@
     def landed(dst, recv):
         pltpu.make_async_copy(dst, dst, recv).wait()
 
+    first, second = pl.ds(0, vir), pl.ds(vir, vir)
+    occ_copy = pltpu.make_async_copy(occ_ref, occ, occ_sem)
+    vir_copy = pltpu.make_async_copy(vir_ref, levels, vir_sem)
     barrier = pltpu.get_barrier_semaphore()
     for xx in range(2):
         for gg in range(groups):
@@ -68,7 +70,7 @@
 
     def ints_copy(c):
         return remote(
-            ints_ref.at[c], ints.at[0, rows(g)], h_send.at[c], h_recv.at[g],
+            ints_ref.at[c], near.at[rows(g), first], h_send.at[c], h_recv.at[g],
             (plane + c % 2, c - c % 2 + x),
         )
 
@@ -80,7 +82,7 @@
 
     def d_copy():
         return remote(
-            ints_ref.at[own_c], ints.at[2, rows(g)], d_send, ring_recv.at[2, g], (ahead, own_c)
+            ints_ref.at[own_c], near.at[rows(g), second], d_send, ring_recv.at[0, g], (ahead, own_c)
         )
 
     d_copy().start()
@@ -91,7 +93,7 @@
 
         @pl.when(to_self(c))
         def _():
-            pltpu.make_async_copy(ints_ref.at[c], ints.at[0, rows(g)], h_recv.at[g]).start()
+            pltpu.make_async_copy(ints_ref.at[c], near.at[rows(g), first], h_recv.at[g]).start()
 
     own_metric = pltpu.make_async_copy(metric_ref, metric.at[rows(g)], own_sem)
     own_metric.start()
@@ -127,22 +129,31 @@
             m3_own(hv).start()
 
     def z_copy(p):
-        return remote(ints.at[0, rows(p)], ints.at[2, rows(p)], z_send.at[p], ring_recv.at[2, p], (ahead, g))
+        return remote(near.at[rows(p), first], near.at[rows(p), second], z_send.at[p], ring_recv.at[0, p], (ahead, g))
 
     def w_copy(p):
-        return remote(ints.at[2, rows(p)], ints.at[3, rows(p)], w_send.at[p], ring_recv.at[3, p], (ahead, mate))
+        return remote(near.at[rows(p), second], far.at[rows(p)], w_send.at[p], ring_recv.at[1, p], (ahead, mate))
 
     def sent_up(p):
         return jnp.logical_not((core == x) & (p // 2 == h))
 
-    def f_copy(src, dst):
-        return remote(fits.at[src], fits.at[dst], f_send.at[dst // 2], f_recv.at[dst // 2], (b, mate))
-
-    levels = jnp.broadcast_to(vir_ref[...], (vir, vir))
-    gap[...] = levels + levels.T
+    def f_copy_all(q):
+        return remote(fit_a.at[span(q)], fit_b.at[span(q)], f_send.at[q], f_recv.at[q], (b, mate))
+
+    def f_copy_one(q):
+        return remote(
+            fit_a.at[span(q), second], fit_b.at[span(q), first], f_send.at[q], f_recv.at[q], (b, mate)
+        )
+
+    occ_copy.start()
+    vir_copy.start()
+    vir_copy.wait()
+    occ_copy.wait()
+    level = jnp.broadcast_to(levels[...], (vir, vir))
+    gap[...] = level + level.T
 
     for p in order:
-        landed(ints.at[0, rows(p)], h_recv.at[p])
+        landed(near.at[rows(p), first], h_recv.at[p])
 
         @pl.when(sent_up(p))
         def _():
@@ -162,7 +173,7 @@
             m3_copy(hv).start()
 
     for p in tail_first:
-        landed(ints.at[2, rows(p)], ring_recv.at[2, p])
+        landed(near.at[rows(p), second], ring_recv.at[0, p])
 
         @pl.when(core == 1)
         def _():
@@ -178,75 +189,63 @@
         def _(q):
             metric_t[span(q), span(p)] = metric[span(p), span(q)].T
 
-    own_energy = occ_ref[own_b * groups + own_c]
-
-    def fit_tile(role, q):
+    own_energy = occ[own_b * groups + own_c]
+
+    def amplitude_of(pair, role):
+        energy = own_energy + occ[(own_b + blocks - role) % blocks * groups + own_c]
+        return ((2.0 * pair.T - pair) / (energy - gap[...])).astype(amp_a.dtype)
+
+    for q in range(tiles):
         low = q * tile
-        fits[role, low:low + tile, :] = jnp.dot(
-            metric_t[low:low + tile, low:], ints[role, low:, :], preferred_element_type=f32,
-        ).astype(fits.dtype)
-
-    def amplitude_of(pair, role):
-        energy = own_energy + occ_ref[(own_b + blocks - role) % blocks * groups + own_c]
-        return ((2.0 * pair.T - pair) / (energy - gap[...])).astype(fits.dtype)
-
-    for role in (0, 2):
-        for q in range(tiles):
-            fit_tile(role, q)
+        fit_a[low:low + tile, :] = jnp.dot(
+            metric_t[low:low + tile, low:], near[low:, :], preferred_element_type=f32,
+        ).astype(fit_a.dtype)
 
         @pl.when(core == 0)
         def _():
-            f_copy(role, role + 1).start()
-
-        if role == 2:
-            @pl.when(core == 1)
-            def _():
-                f_copy(2, 1).start()
-
-    @pl.loop(0, tiles)
-    def _(q):
-        fit_t[:, span(q)] = fits[0, span(q), :].T
-
-    @pl.loop(0, CYCLE - 1)
-    def _(k):
-        role = 2 * k - 3 * (k // 2)
-
-        @pl.when(k == 2)
-        def _():
-            landed(fits.at[1], f_recv.at[0])
-
-        pair = jnp.dot(fit_t[...], fits[role], preferred_element_type=f32)
-        amplitude_t = amplitude_of(pair, role)
-
-        @pl.when(k == 0)
-        def _():
-            dens[...] = jnp.dot(fits[role], amplitude_t, preferred_element_type=f32)
-
-        @pl.when(k > 0)
-        def _():
-            dens[...] += jnp.dot(fits[role], amplitude_t, preferred_element_type=f32)
+            f_copy_all(q).start()
+
+        @pl.when(core == 1)
+        def _():
+            f_copy_one(q).start()
+
+        fit_t[:, low:low + tile] = fit_a[low:low + tile, :vir].T
+
+    pair = jnp.dot(fit_t[...], fit_a[...], preferred_element_type=f32)
+    amp_a[:vir, :] = amplitude_of(pair[:, :vir], 0)
+    amp_a[vir:, :] = amplitude_of(pair[:, vir:], 2)
+    dens[...] = jnp.dot(fit_a[...], amp_a[...], preferred_element_type=f32)
 
     @pl.when(core == 1)
     def _():
-        landed(fits.at[3], f_recv.at[1])
-        pair_sum[...] = jnp.dot(fit_t[...], fits[3], preferred_element_type=f32)
+        for q in range(tiles):
+            landed(fit_b.at[span(q)], f_recv.at[q])
+        pair = jnp.dot(fit_t[...], fit_b[...], preferred_element_type=f32)
+        amp_b[:vir, :] = amplitude_of(pair[:, :vir], 1)
+        amp_b[vir:, :] = amplitude_of(pair[:, vir:], 3)
 
     @pl.when(core == 0)
     def _():
+        for q in range(tiles):
+            landed(fit_b.at[span(q), first], f_recv.at[q])
+        pair = jnp.dot(fit_t[...], fit_b[:, :vir], preferred_element_type=f32)
+        amp_b[:vir, :] = amplitude_of(pair, 1)
+        dens[...] += jnp.dot(fit_b[:, :vir], amp_b[:vir, :], preferred_element_type=f32)
         for q in reversed(range(tiles)):
             low = q * tile
             for p in reversed(range(low // shard, (low + tile) // shard)):
-                landed(ints.at[3, rows(p)], ring_recv.at[3, p])
-            fit_tile(3, q)
+                landed(far.at[rows(p)], ring_recv.at[1, p])
+            fit_b[low:low + tile, vir:] = jnp.dot(
+                metric_t[low:low + tile, low:], far[low:, :], preferred_element_type=f32,
+            ).astype(fit_b.dtype)
             part_sum = jnp.dot(
-                fit_t[:, low:low + tile], fits[3, low:low + tile, :], preferred_element_type=f32
+                fit_t[:, low:low + tile], fit_b[low:low + tile, vir:], preferred_element_type=f32
             )
             if q == tiles - 1:
                 pair_sum[...] = part_sum
             else:
                 pair_sum[...] += part_sum
-
-    amplitude_t = amplitude_of(pair_sum[...], 3)
+        amp_b[vir:, :] = amplitude_of(pair_sum[...], 3)
 
     def g_copy(p):
         return remote(gam.at[rows(p)], out_ref.at[own_c], g_send.at[p], g_recv.at[own_c], (own_b, p))
@@ -256,10 +255,21 @@
 
     for t in range(tiles):
         low = t * tile
-        total = dens[low:low + tile, :] + jnp.dot(
-            fits[3, low:low + tile, :], amplitude_t, preferred_element_type=f32
-        )
-        dens_b[low:low + tile, :] = total.astype(dens_b.dtype)
+
+        @pl.when(core == 0)
+        def _():
+            total = dens[low:low + tile, :] + jnp.dot(
+                fit_b[low:low + tile, vir:], amp_b[vir:, :], preferred_element_type=f32
+            )
+            dens_b[low:low + tile, :] = total.astype(dens_b.dtype)
+
+        @pl.when(core == 1)
+        def _():
+            total = dens[low:low + tile, :] + jnp.dot(
+                fit_b[low:low + tile, :], amp_b[...], preferred_element_type=f32
+            )
+            dens_b[low:low + tile, :] = total.astype(dens_b.dtype)
+
         gam[low:low + tile, :] = jnp.dot(
             metric[low:low + tile, :low + tile], dens_b[:low + tile, :],
             preferred_element_type=f32,
@@ -291,14 +301,14 @@
         def _():
             g_copy(c).wait_send()
 
-    @pl.when(core == 0)
-    def _():
-        f_copy(0, 1).wait_send()
-        f_copy(2, 3).wait_send()
-
-    @pl.when(core == 1)
-    def _():
-        f_copy(2, 1).wait_send()
+    for q in range(tiles):
+        @pl.when(core == 0)
+        def _():
+            f_copy_all(q).wait_send()
+
+        @pl.when(core == 1)
+        def _():
+            f_copy_one(q).wait_send()
 
     for hv in range(pairs):
         @pl.when(h == hv)
@@ -322,7 +332,7 @@
     shard, vir = half_ints.shape[1:]
     naux = metric_inv.shape[1]
     tile = shard if shard % 128 == 0 else naux // 4
-    pairs = groups // 2
+    pairs, tiles = groups // 2, naux // tile
     parts = 4 if shard % 128 == 0 else 1
     dma = pltpu.SemaphoreType.DMA
     return pl.pallas_call(
@@ -331,23 +341,30 @@
         in_specs=[
             pl.BlockSpec(memory_space=pl.ANY),
             pl.BlockSpec(memory_space=pl.ANY),
-            pl.BlockSpec(memory_space=pltpu.SMEM),
-            pl.BlockSpec(memory_space=pltpu.VMEM),
+            pl.BlockSpec(memory_space=pl.ANY),
+            pl.BlockSpec(memory_space=pl.ANY),
         ],
         out_specs=pl.BlockSpec(memory_space=pl.ANY),
         scratch_shapes=[
-            pltpu.VMEM((CYCLE, naux, vir), jnp.bfloat16),
+            pltpu.VMEM((naux, 2 * vir), jnp.bfloat16),
+            pltpu.VMEM((naux, vir), jnp.bfloat16),
             pltpu.VMEM((naux, naux), jnp.bfloat16),
             pltpu.VMEM((naux, naux), jnp.bfloat16),
-            pltpu.VMEM((CYCLE, naux, vir), jnp.bfloat16),
+            pltpu.VMEM((naux, 2 * vir), jnp.bfloat16),
+            pltpu.VMEM((naux, 2 * vir), jnp.bfloat16),
             pltpu.VMEM((vir, naux), jnp.bfloat16),
+            pltpu.VMEM((2 * vir, vir), jnp.bfloat16),
+            pltpu.VMEM((2 * vir, vir), jnp.bfloat16),
             pltpu.VMEM((vir, vir), jnp.float32),
             pltpu.VMEM((vir, vir), jnp.float32),
             pltpu.VMEM((naux, vir), jnp.float32),
             pltpu.VMEM((naux, vir), jnp.bfloat16),
             pltpu.VMEM((naux, vir), jnp.bfloat16),
-            dma((groups,)), dma((groups,)), dma(()), dma((groups,)), dma((groups,)), dma((CYCLE, groups)),
-            dma((2,)), dma((2,)),
+            pltpu.SMEM(occ_energy.shape, jnp.float32),
+            pltpu.VMEM(vir_energy.shape, jnp.float32),
+            dma(()), dma(()),
+            dma((groups,)), dma((groups,)), dma(()), dma((groups,)), dma((groups,)), dma((2, groups)),
+            dma((tiles,)), dma((tiles,)),
             dma((pairs, parts)), dma((pairs, parts)), dma((pairs, parts)), dma((pairs, parts)), dma((pairs,)), dma((pairs,)),
             dma(()), dma((groups,)), dma((groups,)),
         ],

time: 74 us -> 72.6 us (0.981)
  Pallas kernels: 71.4 us -> 70.1 us
    pallas_call x1, Pallas kernels: 71.4 us -> 70.1 us  [local(): pl.pallas_call(functools.partial(kernel, blocks, groups, tile), out_shape...]
where the time goes in v2:
time: 72.6 us; the launch traced here: 72.5 us
  Pallas kernels  70.1 us (97%)
  local copies, waits for them, and re-layouts  2.4 us (3%)
    pallas_call x1, Pallas kernels, local(): pl.pallas_call(functools.partial(kernel, blocks, groups, tile), out_shape...  70.1 us
    unnamed x1, local copies, waits for them, and re-layouts  2.4 us

profile of v2, /device:TPU:0, one launch (start us, length us, event | category | flops | bytes accessed | tf_op | source)
XLA Modules:
  0.0 72.5 jit_solution(17557815567456701310)
XLA Ops:
  0.0 70.1 %shard_map.46 = bf16[4,384,384]{2,1,0:T(8,128)(2,1)} custom-call(bf16[4,384,384]{2,1,0:T(8,128)(2,1)} %ints_ref.1, bf16[384,1536]{1,0:T(8,128)(2,1)} %metric_ref.1, f32[32]{0:T(128)} %occ_ref.1, f32[384]{0:T(512)} %vir_ref.1), custom_call_target="tpu_custom_call" | custom-call | tf_op jit(solution)/shard_map/pallas_call | solution.py:338
  70.1 2.4 %copy.6 = bf16[4,384,384]{2,1,0:T(8,128)(2,1)} copy(bf16[4,384,384]{2,1,0:T(8,128)(2,1)} %shard_map.46) | data formatting | bytes 2359296

commit v3 on v2

--- a/solution.py
+++ b/solution.py
@@ -15,12 +15,12 @@
     ints_ref, metric_ref, occ_ref, vir_ref,
     out_ref,
     near, far, metric, metric_t, fit_a, fit_b, fit_t, amp_a, amp_b, gap, pair_sum, dens, dens_b, gam, occ, levels,
-    occ_sem, vir_sem, h_send, h_recv, d_send, z_send, w_send, ring_recv, f_send, f_recv,
-    m1_send, m1_recv, m2_send, m2_recv, m3_send, m3_recv, own_sem, g_send, g_recv,
+    occ_sem, vir_sem, go, h_send, h_recv, d_send, z_send, w_send, ring_recv, f_send, f_recv,
+    m1_send, m1_recv, m2_send, m2_recv, m3_send, m3_recv, mo_send, mo_recv, own_sem, g_send, g_recv,
 ):
     shard = ints_ref.shape[1]
     half = shard // 2
-    parts = 4 if half % 64 == 0 else 1
+    parts = 6 if half % 96 == 0 else 1
     part = half // parts
     naux = metric_ref.shape[1]
     vir = ints_ref.shape[2]
@@ -36,14 +36,14 @@
     def rows(p):
         return pl.ds(pl.multiple_of(p * shard, shard), shard)
 
-    def slab(p, which, n):
-        return pl.ds(pl.multiple_of(p * shard + which * half + n * part, part), part)
-
     def span(q):
         return pl.ds(pl.multiple_of(q * tile, tile), tile)
 
-    def width(hv):
-        return min(naux, -(-2 * shard * (hv + 1) // tile) * tile)
+    def wide(p, n):
+        return min(naux, -(-(p * shard + 2 * (n + 1) * part) // 128) * 128)
+
+    def tile_end(p):
+        return (p * shard // tile + 1) * tile
 
     def remote(src, dst, send, recv, device):
         return pltpu.make_async_remote_copy(
@@ -78,6 +78,7 @@
         return (core == x) & (c == own_c)
 
     order = [(2 * ((h + r) % pairs) + par) for r in range(pairs) for par in range(2)]
+    last = 2 * ((h + pairs - 1) % pairs) + 1 - x
     tail_first = [groups - 2] + [p for p in range(groups - 1, -1, -1) if p != groups - 2]
 
     def d_copy():
@@ -98,35 +99,72 @@
     own_metric = pltpu.make_async_copy(metric_ref, metric.at[rows(g)], own_sem)
     own_metric.start()
 
-    def m1_copy(hv, r, n):
+    def at_home(act):
+        for hv in range(pairs):
+            for cc in range(2):
+                @pl.when((h == hv) & (core == cc))
+                def _():
+                    act(hv, 2 * hv + cc)
+
+    def away(act):
+        for hv in range(pairs):
+            for cc in range(2):
+                @pl.when((h != hv) & (core == cc))
+                def _():
+                    act(hv, 2 * hv + cc)
+
+    def band(p, which, n):
+        low = pl.multiple_of(p * shard + (2 * n + which) * part, part)
+        return metric.at[pl.ds(low, part), pl.ds(0, wide(p, n))]
+
+    def m1_copy(hv, p, r, n):
+        low = pl.multiple_of((2 * n + x) * part, part)
         return remote(
-            metric_ref.at[slab(0, x, n), pl.ds(0, width(hv))],
-            metric.at[slab(g, x, n), pl.ds(0, width(hv))],
-            m1_send.at[r, n], m1_recv.at[hv, n],
-            (b, 2 * ((h + r) % pairs) + core),
-        )
-
-    def m3_own(hv):
+            metric_ref.at[pl.ds(low, part), pl.ds(0, wide(p, n))], band(p, x, n),
+            m1_send.at[r, n], m1_recv.at[hv, n], (b, 2 * ((h + r) % pairs) + core),
+        )
+
+    def m2_copy(hv, p, n):
+        return remote(band(p, x, n), band(p, x, n), m2_send.at[hv, n], m2_recv.at[hv, n], (across, g))
+
+    def m3_copy(hv, p, own, n):
+        which = x if own else 1 - x
         return remote(
-            metric_ref.at[:, pl.ds(0, width(hv))], metric.at[rows(g), pl.ds(0, width(hv))],
-            m3_send.at[hv], m3_recv.at[hv], (b, mate),
-        )
-
-    def m2_copy(hv, n):
-        piece = metric.at[slab(2 * hv + core, x, n), pl.ds(0, width(hv))]
-        return remote(piece, piece, m2_send.at[hv, n], m2_recv.at[hv, n], (across, g))
-
-    def m3_copy(hv):
-        piece = metric.at[rows(2 * hv + core), pl.ds(0, width(hv))]
-        return remote(piece, piece, m3_send.at[hv], m3_recv.at[hv], (b, mate))
-
-    for hv in range(pairs):
-        @pl.when(h == hv)
-        def _():
-            for r in range(1, pairs):
-                for n in range(parts):
-                    m1_copy(hv, r, n).start()
-            m3_own(hv).start()
+            band(p, which, n), band(p, which, n),
+            m3_send.at[hv, which, n], m3_recv.at[hv, which, n], (b, mate),
+        )
+
+    def home_rows(p):
+        return metric.at[pl.ds(p * shard, shard), pl.ds(0, tile_end(p))]
+
+    def mo_copy(p):
+        return remote(metric_ref.at[:, pl.ds(0, tile_end(p))], home_rows(p), mo_send, mo_recv, (b, mate))
+
+    @at_home
+    def _(hv, p):
+        mo_copy(p).start()
+
+    for p in range(groups):
+        @pl.when(p // 2 != h)
+        def _():
+            for n in range(parts):
+                if wide(p, n) < tile_end(p):
+                    low = p * shard + 2 * n * part
+                    fill = jnp.zeros((2 * part, tile_end(p) - wide(p, n)), metric.dtype)
+                    metric[low:low + 2 * part, wide(p, n):tile_end(p)] = fill
+
+    def m1_step(n):
+        @away
+        def _(hv, p):
+            landed(band(p, x, n), m1_recv.at[hv, n])
+            m2_copy(hv, p, n).start()
+            m3_copy(hv, p, True, n).start()
+
+    def m2_step(n):
+        @away
+        def _(hv, p):
+            landed(band(p, 1 - x, n), m2_recv.at[hv, n])
+            m3_copy(hv, p, False, n).start()
 
     def z_copy(p):
         return remote(near.at[rows(p), first], near.at[rows(p), second], z_send.at[p], ring_recv.at[0, p], (ahead, g))
@@ -152,42 +190,91 @@
     level = jnp.broadcast_to(levels[...], (vir, vir))
     gap[...] = level + level.T
 
-    for p in order:
-        landed(near.at[rows(p), first], h_recv.at[p])
-
-        @pl.when(sent_up(p))
-        def _():
-            z_copy(p).start()
-
-    for hv in range(pairs):
-        @pl.when(h != hv)
-        def _():
-            for n in range(parts):
-                landed(metric.at[slab(2 * hv + core, x, n), pl.ds(0, width(hv))], m1_recv.at[hv, n])
-                m2_copy(hv, n).start()
-    for hv in range(pairs):
-        @pl.when(h != hv)
-        def _():
-            for n in range(parts):
-                landed(metric.at[slab(2 * hv + core, 1 - x, n), pl.ds(0, width(hv))], m2_recv.at[hv, n])
-            m3_copy(hv).start()
-
-    for p in tail_first:
-        landed(near.at[rows(p), second], ring_recv.at[0, p])
-
-        @pl.when(core == 1)
-        def _():
-            w_copy(p).start()
-
     own_metric.wait()
-    for hv in range(pairs):
-        landed(metric.at[rows(2 * hv + 1 - core), pl.ds(0, width(hv))], m3_recv.at[hv])
-
-    @pl.loop(0, tiles)
-    def _(p):
+
+    @at_home
+    def _(hv, p):
+        landed(home_rows(p + 1 - 2 * (p % 2)), mo_recv)
+
+    def turn(p):
         @pl.loop(0, p + 1)
         def _(q):
             metric_t[span(q), span(p)] = metric[span(p), span(q)].T
+
+    if tile == shard:
+        turn(2 * h)
+        turn(2 * h + 1)
+
+    def pass_own(p):
+        landed(near.at[rows(p), first], h_recv.at[p])
+
+        @pl.when(sent_up(p))
+        def _():
+            z_copy(p).start()
+
+    def pass_on(p):
+        landed(near.at[rows(p), second], ring_recv.at[0, p])
+
+        @pl.when(core == 1)
+        def _():
+            w_copy(p).start()
+
+    for p in order[:2]:
+        pass_own(p)
+
+    @at_home
+    def _(hv, p):
+        for n in range(parts // 2):
+            for r in range(1, pairs):
+                m1_copy(hv, p, r, n).start()
+
+    for p in order[2:3]:
+        pass_own(p)
+    ints_copy(last).wait_send()
+
+    @at_home
+    def _(hv, p):
+        for n in range(parts // 2, parts):
+            for r in range(1, pairs):
+                m1_copy(hv, p, r, n).start()
+
+    for p in order[3:]:
+        pass_own(p)
+    for n in range(parts):
+        m1_step(n)
+        if n >= 2:
+            m2_step(n - 2)
+    @pl.when(core == 0)
+    def _():
+        for p in range(groups):
+            @pl.when(sent_up(p))
+            def _():
+                z_copy(p).wait_send()
+        pl.semaphore_signal(go, inc=1, device_id=(b, mate), device_id_type=MESH)
+
+    @pl.when(core == 1)
+    def _():
+        pl.semaphore_wait(go, 1)
+
+    pass_on(tail_first[0])
+    for n in range(max(parts - 2, 0), parts):
+        m2_step(n)
+    for p in tail_first[1:]:
+        pass_on(p)
+
+    @away
+    def _(hv, p):
+        other = p + 1 - 2 * (p % 2)
+        for n in range(parts):
+            landed(band(other, 0, n), m3_recv.at[hv, 0, n])
+            landed(band(other, 1, n), m3_recv.at[hv, 1, n])
+
+    if tile == shard:
+        for r in range(1, pairs):
+            turn(2 * ((h + r) % pairs))
+            turn(2 * ((h + r) % pairs) + 1)
+    else:
+        pl.loop(0, tiles)(turn)
 
     own_energy = occ[own_b * groups + own_c]
 
@@ -285,11 +372,11 @@
 
     d_copy().wait_send()
     for c in range(groups):
-        @pl.when(jnp.logical_not(to_self(c)))
+        @pl.when(jnp.logical_not(to_self(c)) & (c != last))
         def _():
             ints_copy(c).wait_send()
 
-        @pl.when(sent_up(c))
+        @pl.when(sent_up(c) & (core == 1))
         def _():
             z_copy(c).wait_send()
 
@@ -310,19 +397,20 @@
         def _():
             f_copy_one(q).wait_send()
 
-    for hv in range(pairs):
-        @pl.when(h == hv)
-        def _():
+    @at_home
+    def _(hv, p):
+        for n in range(parts):
             for r in range(1, pairs):
-                for n in range(parts):
-                    m1_copy(hv, r, n).wait_send()
-            m3_own(hv).wait_send()
-
-        @pl.when(h != hv)
-        def _():
-            for n in range(parts):
-                m2_copy(hv, n).wait_send()
-            m3_copy(hv).wait_send()
+                m1_copy(hv, p, r, n).wait_send()
+        mo_copy(p).wait_send()
+
+    @away
+    def _(hv, p):
+        for n in range(parts):
+            m2_copy(hv, p, n).wait_send()
+            m3_copy(hv, p, True, n).wait_send()
+            m3_copy(hv, p, False, n).wait_send()
+
     for c in range(groups):
         landed(out_ref.at[c], g_recv.at[c])
 
@@ -333,7 +421,7 @@
     naux = metric_inv.shape[1]
     tile = shard if shard % 128 == 0 else naux // 4
     pairs, tiles = groups // 2, naux // tile
-    parts = 4 if shard % 128 == 0 else 1
+    parts = 6 if shard % 192 == 0 else 1
     dma = pltpu.SemaphoreType.DMA
     return pl.pallas_call(
         functools.partial(kernel, blocks, groups, tile),
@@ -362,10 +450,11 @@
             pltpu.VMEM((naux, vir), jnp.bfloat16),
             pltpu.SMEM(occ_energy.shape, jnp.float32),
             pltpu.VMEM(vir_energy.shape, jnp.float32),
-            dma(()), dma(()),
+            dma(()), dma(()), pltpu.SemaphoreType.REGULAR,
             dma((groups,)), dma((groups,)), dma(()), dma((groups,)), dma((groups,)), dma((2, groups)),
             dma((tiles,)), dma((tiles,)),
-            dma((pairs, parts)), dma((pairs, parts)), dma((pairs, parts)), dma((pairs, parts)), dma((pairs,)), dma((pairs,)),
+            dma((pairs, parts)), dma((pairs, parts)), dma((pairs, parts)), dma((pairs, parts)),
+            dma((pairs, 2, parts)), dma((pairs, 2, parts)), dma(()), dma(()),
             dma(()), dma((groups,)), dma((groups,)),
         ],
         compiler_params=pltpu.CompilerParams(

time: 72.6 us -> 70.2 us (0.967)
  Pallas kernels: 70.1 us -> 67.6 us
    pallas_call x1, Pallas kernels: 70.1 us -> 67.6 us  [local(): pl.pallas_call(functools.partial(kernel, blocks, groups, tile), out_shape...]
where the time goes in v3:
time: 70.2 us; the launch traced here: 70.1 us
  Pallas kernels  67.6 us (96%)
  local copies, waits for them, and re-layouts  2.4 us (3%)
    pallas_call x1, Pallas kernels, local(): pl.pallas_call(functools.partial(kernel, blocks, groups, tile), out_shape...  67.6 us
    unnamed x1, local copies, waits for them, and re-layouts  2.4 us

profile of v3, /device:TPU:0, one launch (start us, length us, event | category | flops | bytes accessed | tf_op | source)
XLA Modules:
  0.0 70.1 jit_solution(5349765395928646128)
XLA Ops:
  0.0 67.6 %shard_map.46 = bf16[4,384,384]{2,1,0:T(8,128)(2,1)} custom-call(bf16[4,384,384]{2,1,0:T(8,128)(2,1)} %ints_ref.1, bf16[384,1536]{1,0:T(8,128)(2,1)} %metric_ref.1, f32[32]{0:T(128)} %occ_ref.1, f32[384]{0:T(512)} %vir_ref.1), custom_call_target="tpu_custom_call" | custom-call | tf_op jit(solution)/shard_map/pallas_call | solution.py:426
  67.7 2.4 %copy.6 = bf16[4,384,384]{2,1,0:T(8,128)(2,1)} copy(bf16[4,384,384]{2,1,0:T(8,128)(2,1)} %shard_map.46) | data formatting | bytes 2359296

commit v4 on v3

--- a/solution.py
+++ b/solution.py
@@ -15,7 +15,7 @@
     ints_ref, metric_ref, occ_ref, vir_ref,
     out_ref,
     near, far, metric, metric_t, fit_a, fit_b, fit_t, amp_a, amp_b, gap, pair_sum, dens, dens_b, gam, occ, levels,
-    occ_sem, vir_sem, go, h_send, h_recv, d_send, z_send, w_send, ring_recv, f_send, f_recv,
+    occ_sem, vir_sem, go, h_send, h_recv, d_send, z_send, w_send, ring_recv, far_recv, f_send, f_recv,
     m1_send, m1_recv, m2_send, m2_recv, m3_send, m3_recv, mo_send, mo_recv, own_sem, g_send, g_recv,
 ):
     shard = ints_ref.shape[1]
@@ -68,10 +68,13 @@
             pl.semaphore_signal(barrier, inc=1, device_id=(bb, gg), device_id_type=MESH)
     pl.semaphore_wait(barrier, 2 * groups + 3)
 
-    def ints_copy(c):
-        return remote(
-            ints_ref.at[c], near.at[rows(g), first], h_send.at[c], h_recv.at[g],
-            (plane + c % 2, c - c % 2 + x),
+    def strip(p, k):
+        return pl.ds(pl.multiple_of(p * shard + k * half, half), half)
+
+    def ints_copy(c, k):
+        return remote(
+            ints_ref.at[c, pl.ds(k * half, half)], near.at[strip(g, k), first],
+            h_send.at[c, k], h_recv.at[g, k], (plane + c % 2, c - c % 2 + x),
         )
 
     def to_self(c):
@@ -81,20 +84,26 @@
     last = 2 * ((h + pairs - 1) % pairs) + 1 - x
     tail_first = [groups - 2] + [p for p in range(groups - 1, -1, -1) if p != groups - 2]
 
-    def d_copy():
-        return remote(
-            ints_ref.at[own_c], near.at[rows(g), second], d_send, ring_recv.at[0, g], (ahead, own_c)
-        )
-
-    d_copy().start()
+    def d_copy(k):
+        return remote(
+            ints_ref.at[own_c, pl.ds(k * half, half)], near.at[strip(g, k), second],
+            d_send.at[k], ring_recv.at[g, k], (ahead, own_c),
+        )
+
+    for k in range(2):
+        d_copy(k).start()
     for c in order:
         @pl.when(jnp.logical_not(to_self(c)))
         def _():
-            ints_copy(c).start()
+            for k in range(2):
+                ints_copy(c, k).start()
 
         @pl.when(to_self(c))
         def _():
-            pltpu.make_async_copy(ints_ref.at[c], near.at[rows(g), first], h_recv.at[g]).start()
+            for k in range(2):
+                pltpu.make_async_copy(
+                    ints_ref.at[c, pl.ds(k * half, half)], near.at[strip(g, k), first], h_recv.at[g, k]
+                ).start()
 
     own_metric = pltpu.make_async_copy(metric_ref, metric.at[rows(g)], own_sem)
     own_metric.start()
@@ -166,11 +175,14 @@
             landed(band(p, 1 - x, n), m2_recv.at[hv, n])
             m3_copy(hv, p, False, n).start()
 
-    def z_copy(p):
-        return remote(near.at[rows(p), first], near.at[rows(p), second], z_send.at[p], ring_recv.at[0, p], (ahead, g))
+    def z_copy(p, k):
+        return remote(
+            near.at[strip(p, k), first], near.at[strip(p, k), second],
+            z_send.at[p, k], ring_recv.at[p, k], (ahead, g),
+        )
 
     def w_copy(p):
-        return remote(near.at[rows(p), second], far.at[rows(p)], w_send.at[p], ring_recv.at[1, p], (ahead, mate))
+        return remote(near.at[rows(p), second], far.at[rows(p)], w_send.at[p], far_recv.at[p], (ahead, mate))
 
     def sent_up(p):
         return jnp.logical_not((core == x) & (p // 2 == h))
@@ -206,14 +218,16 @@
         turn(2 * h + 1)
 
     def pass_own(p):
-        landed(near.at[rows(p), first], h_recv.at[p])
-
-        @pl.when(sent_up(p))
-        def _():
-            z_copy(p).start()
+        for k in range(2):
+            landed(near.at[strip(p, k), first], h_recv.at[p, k])
+
+            @pl.when(sent_up(p))
+            def _():
+                z_copy(p, k).start()
 
     def pass_on(p):
-        landed(near.at[rows(p), second], ring_recv.at[0, p])
+        for k in range(2):
+            landed(near.at[strip(p, k), second], ring_recv.at[p, k])
 
         @pl.when(core == 1)
         def _():
@@ -230,7 +244,8 @@
 
     for p in order[2:3]:
         pass_own(p)
-    ints_copy(last).wait_send()
+    for k in range(2):
+        ints_copy(last, k).wait_send()
 
     @at_home
     def _(hv, p):
@@ -246,10 +261,11 @@
             m2_step(n - 2)
     @pl.when(core == 0)
     def _():
-        for p in range(groups):
+        for p in order[:-1]:
             @pl.when(sent_up(p))
             def _():
-                z_copy(p).wait_send()
+                for k in range(2):
+                    z_copy(p, k).wait_send()
         pl.semaphore_signal(go, inc=1, device_id=(b, mate), device_id_type=MESH)
 
     @pl.when(core == 1)
@@ -321,7 +337,7 @@
         for q in reversed(range(tiles)):
             low = q * tile
             for p in reversed(range(low // shard, (low + tile) // shard)):
-                landed(far.at[rows(p)], ring_recv.at[1, p])
+                landed(far.at[rows(p)], far_recv.at[p])
             fit_b[low:low + tile, vir:] = jnp.dot(
                 metric_t[low:low + tile, low:], far[low:, :], preferred_element_type=f32,
             ).astype(fit_b.dtype)
@@ -370,15 +386,25 @@
             def _():
                 pltpu.make_async_copy(gam.at[rows(p)], out_ref.at[own_c], g_recv.at[own_c]).start()
 
-    d_copy().wait_send()
+    for k in range(2):
+        d_copy(k).wait_send()
+
+    @pl.when(core == 0)
+    def _():
+        for p in order[-1:]:
+            for k in range(2):
+                z_copy(p, k).wait_send()
+
     for c in range(groups):
         @pl.when(jnp.logical_not(to_self(c)) & (c != last))
         def _():
-            ints_copy(c).wait_send()
+            for k in range(2):
+                ints_copy(c, k).wait_send()
 
         @pl.when(sent_up(c) & (core == 1))
         def _():
-            z_copy(c).wait_send()
+            for k in range(2):
+                z_copy(c, k).wait_send()
 
         @pl.when(core == 1)
         def _():
@@ -451,7 +477,7 @@
             pltpu.SMEM(occ_energy.shape, jnp.float32),
             pltpu.VMEM(vir_energy.shape, jnp.float32),
             dma(()), dma(()), pltpu.SemaphoreType.REGULAR,
-            dma((groups,)), dma((groups,)), dma(()), dma((groups,)), dma((groups,)), dma((2, groups)),
+            dma((groups, 2)), dma((groups, 2)), dma((2,)), dma((groups, 2)), dma((groups,)), dma((groups, 2)), dma((groups,)),
             dma((tiles,)), dma((tiles,)),
             dma((pairs, parts)), dma((pairs, parts)), dma((pairs, parts)), dma((pairs, parts)),
             dma((pairs, 2, parts)), dma((pairs, 2, parts)), dma(()), dma(()),

time: 70.2 us -> 69.2 us (0.986)
  Pallas kernels: 67.6 us -> 66.6 us
    pallas_call x1, Pallas kernels: 67.6 us -> 66.6 us  [local(): pl.pallas_call(functools.partial(kernel, blocks, groups, tile), out_shape...]
where the time goes in v4:
time: 69.2 us; the launch traced here: 69 us
  Pallas kernels  66.6 us (96%)
  local copies, waits for them, and re-layouts  2.4 us (3%)
    pallas_call x1, Pallas kernels, local(): pl.pallas_call(functools.partial(kernel, blocks, groups, tile), out_shape...  66.6 us
    unnamed x1, local copies, waits for them, and re-layouts  2.4 us

profile of v4, /device:TPU:0, one launch (start us, length us, event | category | flops | bytes accessed | tf_op | source)
XLA Modules:
  0.0 69.0 jit_solution(2372799817141021942)
XLA Ops:
  0.0 66.6 %shard_map.46 = bf16[4,384,384]{2,1,0:T(8,128)(2,1)} custom-call(bf16[4,384,384]{2,1,0:T(8,128)(2,1)} %ints_ref.1, bf16[384,1536]{1,0:T(8,128)(2,1)} %metric_ref.1, f32[32]{0:T(128)} %occ_ref.1, f32[384]{0:T(512)} %vir_ref.1), custom_call_target="tpu_custom_call" | custom-call | tf_op jit(solution)/shard_map/pallas_call | solution.py:452
  66.6 2.4 %copy.6 = bf16[4,384,384]{2,1,0:T(8,128)(2,1)} copy(bf16[4,384,384]{2,1,0:T(8,128)(2,1)} %shard_map.46) | data formatting | bytes 2359296

commit v5 on v4

--- a/solution.py
+++ b/solution.py
@@ -441,6 +441,17 @@
         landed(out_ref.at[c], g_recv.at[c])
 
 
+def hand_over(gam_ref, out_ref, held, in_sem, out_sem):
+    units = gam_ref.shape[0]
+    for c in range(units):
+        pltpu.make_async_copy(gam_ref.at[c], held.at[c], in_sem.at[c]).start()
+    for c in range(units):
+        pltpu.make_async_copy(gam_ref.at[c], held.at[c], in_sem.at[c]).wait()
+        pltpu.make_async_copy(held.at[c], out_ref.at[c], out_sem.at[c]).start()
+    for c in range(units):
+        pltpu.make_async_copy(held.at[c], out_ref.at[c], out_sem.at[c]).wait()
+
+
 def local(half_ints, metric_inv, occ_energy, vir_energy):
     groups, blocks = lax.axis_size("aux"), lax.axis_size("blk")
     shard, vir = half_ints.shape[1:]
@@ -449,7 +460,7 @@
     pairs, tiles = groups // 2, naux // tile
     parts = 6 if shard % 192 == 0 else 1
     dma = pltpu.SemaphoreType.DMA
-    return pl.pallas_call(
+    gamma = pl.pallas_call(
         functools.partial(kernel, blocks, groups, tile),
         out_shape=jax.ShapeDtypeStruct(half_ints.shape, jnp.bfloat16),
         in_specs=[
@@ -487,6 +498,13 @@
             collective_id=0, has_side_effects=True, vmem_limit_bytes=56 * 2**20
         ),
     )(half_ints, metric_inv, occ_energy, vir_energy)
+    return pl.pallas_call(
+        hand_over,
+        out_shape=jax.ShapeDtypeStruct(half_ints.shape, jnp.bfloat16),
+        in_specs=[pl.BlockSpec(memory_space=pl.ANY)],
+        out_specs=pl.BlockSpec(memory_space=pl.ANY),
+        scratch_shapes=[pltpu.VMEM(half_ints.shape, jnp.bfloat16), dma((groups,)), dma((groups,))],
+    )(gamma)
 
 
 def solution(mesh):

time: 69.2 us -> 68.9 us (level)
  local copies, waits for them, and re-layouts: 2.4 us -> 0 us
  Pallas kernels: 66.6 us -> 68.6 us
    unnamed x1 -> x0, local copies, waits for them, and re-layouts: 2.4 us -> none
    pallas_call x0 -> x1, Pallas kernels: none -> 2.04 us  [local(): pl.pallas_call(hand_over, out_shape=jax.ShapeDtypeStruct(half_ints.shape,...]
where the time goes in v5:
time: 68.9 us; the launch traced here: 68.8 us
  Pallas kernels  68.6 us (100%)
    pallas_call x1, Pallas kernels, local(): pl.pallas_call(functools.partial(kernel, blocks, groups, tile), out_shape...  66.6 us
    pallas_call x1, Pallas kernels, local(): pl.pallas_call(hand_over, out_shape=jax.ShapeDtypeStruct(half_ints.shape,...  2.04 us

profile of v5, /device:TPU:0, one launch (start us, length us, event | category | flops | bytes accessed | tf_op | source)
XLA Modules:
  0.0 68.8 jit_solution(1776524304900438802)
XLA Ops:
  0.0 66.6 %shard_map.46.gam_ref = bf16[4,384,384]{2,1,0:T(8,128)(2,1)} custom-call(bf16[4,384,384]{2,1,0:T(8,128)(2,1)} %ints_ref.1, bf16[384,1536]{1,0:T(8,128)(2,1)} %metric_ref.1, f32[32]{0:T(128)} %occ_ref.1, f32[384]{0:T(512)} %vir_ref.1), custom_call_target="tpu_custom_call" | custom-call | tf_op jit(solution)/shard_map/pallas_call | solution.py:463
  66.6 2.0 %shard_map.47 = bf16[4,384,384]{2,1,0:T(8,128)(2,1)} custom-call(bf16[4,384,384]{2,1,0:T(8,128)(2,1)} %shard_map.46.gam_ref), custom_call_target="tpu_custom_call" | custom-call | tf_op jit(solution)/shard_map/pallas_call | solution.py:501

commit v6 on v5

--- a/solution.py
+++ b/solution.py
@@ -14,7 +14,7 @@
     blocks, groups, tile,
     ints_ref, metric_ref, occ_ref, vir_ref,
     out_ref,
-    near, far, metric, metric_t, fit_a, fit_b, fit_t, amp_a, amp_b, gap, pair_sum, dens, dens_b, gam, occ, levels,
+    near, far, metric, metric_t, fit_a, fit_b, fit_t, amp_a, amp_b, gap, pair_sum, carry, dens, dens_b, gam, occ, levels,
     occ_sem, vir_sem, go, h_send, h_recv, d_send, z_send, w_send, ring_recv, far_recv, f_send, f_recv,
     m1_send, m1_recv, m2_send, m2_recv, m3_send, m3_recv, mo_send, mo_recv, own_sem, g_send, g_recv,
 ):
@@ -336,11 +336,18 @@
         dens[...] += jnp.dot(fit_b[:, :vir], amp_b[:vir, :], preferred_element_type=f32)
         for q in reversed(range(tiles)):
             low = q * tile
+            if q < tiles - 1:
+                carry[...] = jnp.dot(
+                    metric_t[low:low + tile, low + tile:], far[low + tile:, :], preferred_element_type=f32
+                )
             for p in reversed(range(low // shard, (low + tile) // shard)):
                 landed(far.at[rows(p)], far_recv.at[p])
-            fit_b[low:low + tile, vir:] = jnp.dot(
-                metric_t[low:low + tile, low:], far[low:, :], preferred_element_type=f32,
-            ).astype(fit_b.dtype)
+            block = jnp.dot(
+                metric_t[low:low + tile, low:low + tile], far[low:low + tile, :], preferred_element_type=f32
+            )
+            if q < tiles - 1:
+                block += carry[...]
+            fit_b[low:low + tile, vir:] = block.astype(fit_b.dtype)
             part_sum = jnp.dot(
                 fit_t[:, low:low + tile], fit_b[low:low + tile, vir:], preferred_element_type=f32
             )
@@ -482,6 +489,7 @@
             pltpu.VMEM((2 * vir, vir), jnp.bfloat16),
             pltpu.VMEM((vir, vir), jnp.float32),
             pltpu.VMEM((vir, vir), jnp.float32),
+            pltpu.VMEM((tile, vir), jnp.float32),
             pltpu.VMEM((naux, vir), jnp.float32),
             pltpu.VMEM((naux, vir), jnp.bfloat16),
             pltpu.VMEM((naux, vir), jnp.bfloat16),

time: 68.9 us -> 68.9 us (level)
  no operation moved by 1% of the time
where the time goes in v6:
time: 68.9 us; the launch traced here: 68.7 us
  Pallas kernels  68.6 us (100%)
    pallas_call x1, Pallas kernels, local(): pl.pallas_call(functools.partial(kernel, blocks, groups, tile), out_shape...  66.5 us
    pallas_call x1, Pallas kernels, local(): pl.pallas_call(hand_over, out_shape=jax.ShapeDtypeStruct(half_ints.shape,...  2.04 us

profile of v6, /device:TPU:0, one launch (start us, length us, event | category | flops | bytes accessed | tf_op | source)
XLA Modules:
  0.0 68.7 jit_solution(2971119608055750668)
XLA Ops:
  0.0 66.5 %shard_map.46.gam_ref = bf16[4,384,384]{2,1,0:T(8,128)(2,1)} custom-call(bf16[4,384,384]{2,1,0:T(8,128)(2,1)} %ints_ref.1, bf16[384,1536]{1,0:T(8,128)(2,1)} %metric_ref.1, f32[32]{0:T(128)} %occ_ref.1, f32[384]{0:T(512)} %vir_ref.1), custom_call_target="tpu_custom_call" | custom-call | tf_op jit(solution)/shard_map/pallas_call | solution.py:470
  66.5 2.0 %shard_map.47 = bf16[4,384,384]{2,1,0:T(8,128)(2,1)} custom-call(bf16[4,384,384]{2,1,0:T(8,128)(2,1)} %shard_map.46.gam_ref), custom_call_target="tpu_custom_call" | custom-call | tf_op jit(solution)/shard_map/pallas_call | solution.py:509
